TPU v7x, 32 devices: a whole 2x2x4 slice. The times are simulated.
32 devices in a mesh: layer: 4 (over x, core), ex: 8 (over z, y).
Axes of the slice: x: 2, y: 2, z: 4, core: 2. Of those that a mesh axis runs over, the one named last changes fastest.
Arguments:
- queries: bfloat16 [128, 8, 4096], P('ex', 'layer'), may hold values from -6 to 6
- stored: bfloat16 [2048, 8, 4096], P('ex', 'layer'), may hold values from -0.03125 to 0.03125
- left_inv: bfloat16 [8, 64, 64], P('layer'), may hold values from -0.078125 to 2
- right_inv: bfloat16 [8, 64, 64], P('layer'), may hold values from -0.078125 to 2
Outputs:
- scores: float32 [128, 2048], P('layer', 'ex')
All inputs are finite; a program needn't handle non-finite values.
Results may differ from a plain program's by a relative error of at most 0.0041.
Values may be sent and summed in bfloat16 or wider, within the bound.
A program may use at most 128 MiB of HBM per device.

v0:
```python
import jax
import jax.numpy as jnp
from jax import lax
from jax.sharding import PartitionSpec as P


def precondition(gradients, left_inv, right_inv):
    count = gradients.shape[0]
    layers_here = gradients.shape[1]
    side = left_inv.shape[1]
    mats = gradients.reshape(count, layers_here, side, side)
    left_side = jnp.einsum(
        "lia,qlaj->qlij", left_inv, mats, preferred_element_type=jnp.float32
    ).astype(jnp.bfloat16)
    ready = jnp.einsum(
        "qlib,lbj->qlij", left_side, right_inv, preferred_element_type=jnp.float32
    ).astype(jnp.bfloat16)
    return ready.reshape(count, layers_here * side * side)


def shards(queries, stored, left_inv, right_inv):
    stored_flat = stored.reshape(stored.shape[0], stored.shape[1] * stored.shape[2])
    own_ready = precondition(queries, left_inv, right_inv)
    partial_value = lax.dot_general(
        lax.all_gather(own_ready, "ex", axis=0, tiled=True),
        stored_flat,
        (((1,), (1,)), ((), ())),
        preferred_element_type=jnp.float32,
    )
    return lax.psum_scatter(partial_value, "layer", scatter_dimension=0, tiled=True)


def solution(mesh):
    placed = (
        P("ex", "layer", None),
        P("ex", "layer", None),
        P("layer", None, None),
        P("layer", None, None),
    )
    return jax.shard_map(
        shards, mesh=mesh, in_specs=placed, out_specs=P("layer", "ex"), check_vma=False
    )
```

profile of v0, /device:TPU:0, one launch (start us, length us, event | category | flops | bytes accessed | tf_op | source)
XLA Modules:
  0.0 92.5 jit_solution(12882949968957154672)
XLA Ops:
  6.5 0.0 copy-start
  6.5 0.0 all-gather.2.cloned.1.call-start
  6.5 1.3 %reshape.9 = bf16[16,2,64,64]{3,2,1,0:T(8,128)(2,1)S(1)} reshape(bf16[16,2,4096]{2,1,0:T(2,128)(2,1)} %param.4) | data formatting | bytes 524288 | tf_op jit(solution)/shard_map/reshape | solution.py:11
  7.9 0.0 copy-done
  7.9 1.2 %fusion = bf16[16,2,64,64]{3,2,0,1:T(8,128)(2,1)S(1)} fusion(bf16[16,2,64,64]{3,2,1,0:T(8,128)(2,1)S(1)} %reshape.9, bf16[2,64,64]{2,1,0:T(8,128)(2,1)S(1)} %copy-done, bf16[2,64,64]{2,1,0:T(8,128)(2,1)} %param.6), kind=kOutput, calls=%fused_computation.2 | convolution fusion | flops 33816576 | bytes 557056 | tf_op jit(solution)/shard_map/qlib,lbj->qlij/dot_general | solution.py:15
  9.2 1.2 %reshape.10 = bf16[16,8192]{1,0:T(8,128)(2,1)} reshape(bf16[16,2,64,64]{3,2,1,0:T(8,128)(2,1)S(1)} %copy.5) | data formatting | bytes 524288 | tf_op jit(solution)/shard_map/reshape | solution.py:18
  10.3 0.0 all-gather.2.cloned.1.call-update
  10.4 0.0 reduce-scatter.2.cloned.1.call-start
  10.4 8.6 %copy.9 = bf16[32,8,2,4096]{3,1,2,0:T(8,128)(2,1)} copy(bf16[32,8,2,4096]{3,2,1,0:T(2,128)(2,1)} %bitcast.24) | data formatting | bytes 8388608
  19.0 43.3 %all-gather.2.cloned.1.call-done = bf16[128,8192]{1,0:T(8,128)(2,1)} async-done(((bf16[16,8192]{1,0:T(8,128)(2,1)}), bf16[128,8192]{1,0:T(8,128)(2,1)}) %all-gather.2.cloned.1.call-update) | async-done | bytes 2097168 | tf_op jit(solution)/shard_map/all_gather | solution.py:25
  62.3 5.0 %fusion.7 = f32[128,256]{1,0:T(8,128)} fusion(bf16[128,8192]{1,0:T(8,128)(2,1)} %all-gather.2.cloned.1.call-done, bf16[256,8192]{1,0:T(8,128)(2,1)} %bitcast.23), kind=kOutput, calls=%fused_computation.7 | convolution fusion | flops 536870912 | bytes 6422528 | tf_op jit(solution)/shard_map/dot_general | solution.py:24
  67.3 0.0 reduce-scatter.2.cloned.1.call-update
  67.4 18.3 %reduce-scatter.2.cloned.1.call-done = f32[32,256]{1,0:T(8,128)} async-done(((f32[128,256]{1,0:T(8,128)}), f32[32,256]{1,0:T(8,128)}) %reduce-scatter.2.cloned.1.call-update) | async-done | bytes 32784 | tf_op jit(solution)/shard_map/reduce_scatter | solution.py:30
  (1 shorter events, 0.0 us)
Async XLA Ops:
  6.5 1.4 %copy-start = (bf16[2,64,64]{2,1,0:T(8,128)(2,1)S(1)}, bf16[2,64,64]{2,1,0:T(8,128)(2,1)}, u32[]{:S(2)}) copy-start(bf16[2,64,64]{2,1,0:T(8,128)(2,1)} %param.7) | copy-start | bytes 49156
  6.5 55.8 %all-gather.2.cloned.1.call-start = ((), (), s32[]{:S(2)}) async-start(), calls=%async_computation.1 | async-start | bytes 2359296 | tf_op jit(solution)/shard_map/all_gather | solution.py:25
  10.4 75.3 %reduce-scatter.2.cloned.1.call-start = ((), (), s32[]{:S(2)}) async-start(), calls=%async_computation.2 | async-start | bytes 163840 | tf_op jit(solution)/shard_map/reduce_scatter | solution.py:30
Sparse Core Ops, SparseCore 0:
  10.5 51.7 all-gather.1
  67.5 18.1 reduce-scatter.1
where the time goes:
time: 92.8 us; the launch traced here: 92.5 us
  waiting for transfers between devices  61.6 us (66%)
  between operations  13.4 us (14%)
  local copies, waits for them, and re-layouts  11.2 us (12%)
  matrix products  6.23 us (7%)
    all_gather x1, waiting for transfers between devices, shards(): lax.all_gather(own_ready, 'ex', axis=0, tiled=True)  43.3 us
    reduce_scatter x1, waiting for transfers between devices, shards(): lax.psum_scatter(partial_value, 'layer', scatter_dimension=0, tiled=True)  18.3 us
    unnamed x3, local copies, waits for them, and re-layouts  8.62 us
    dot_general x1, matrix products, shards(): lax.dot_general(lax.all_gather(own_ready, 'ex', axis=0, tiled=True), stor...  5.01 us
  transfers between devices with their start and end apart: 2, of which 2 were waited for; matrix products, arithmetic and copies ran while one was open for 9% of the time, Pallas kernels for 0%

commit v1 on v0

v1 whole, which is shorter than its diff:
```python
import functools

import jax
import jax.numpy as jnp
from jax import lax
from jax.experimental import pallas as pl
from jax.experimental.pallas import tpu as pltpu
from jax.sharding import PartitionSpec as P

MESH = pl.DeviceIdType.MESH
LANES = 128
F32 = jnp.float32
BF16 = jnp.bfloat16


def iota(shape, axis):
    return lax.broadcasted_iota(jnp.int32, shape, axis)


def one_hot(mask):
    return jnp.where(mask, 1.0, 0.0).astype(BF16)


def dot(a, b):
    return jnp.dot(a, b, preferred_element_type=F32)


def kernel(
    groups, ex, per_block, layers_here, side, parts,
    q_hbm, s_hbm, l_ref, r_ref, out_ref,
    gathered, raw, flat_stored, lifted, left_mat, right_mat, ready_wide, ready_flat,
    partial, arrived,
    got, sent_up, sent_down, sent_across, own_sem, raw_sem, out_sem, in_sem,
):
    layer = lax.axis_index("layer")
    me = lax.axis_index("ex")
    depth = ex // 2
    z, y = me // 2, me % 2
    per = LANES // side
    tiles = side // per
    rows = tiles * layers_here
    piece = per_block // parts

    barrier = pltpu.get_barrier_semaphore()

    def greet(**where):
        pl.semaphore_signal(barrier, inc=1, device_id=where, device_id_type=MESH)

    pl.when(z > 0)(lambda: greet(ex=me - 2))
    pl.when(z < depth - 1)(lambda: greet(ex=me + 2))
    greet(ex=me + 1 - 2 * y)
    for step in range(1, groups):
        greet(layer=lax.rem(layer + step, groups))

    own_copy = pltpu.make_async_copy(q_hbm, gathered.at[me], own_sem)
    own_copy.start()
    n_raw = raw_sem.shape[0]
    stored_rows = raw.shape[0]
    raw_rows = stored_rows // n_raw

    def raw_copy(i):
        at = pl.ds(i * raw_rows, raw_rows)
        return pltpu.make_async_copy(s_hbm.at[at], raw.at[at], raw_sem.at[i])

    for i in range(n_raw):
        raw_copy(i).start()

    here = (z > 0).astype(jnp.int32) + (z < depth - 1).astype(jnp.int32)
    pl.semaphore_wait(barrier, here + groups)

    def hop(block, h, sem, target, source=None):
        at = pl.ds(h * piece, piece)
        return pltpu.make_async_remote_copy(
            src_ref=gathered.at[block, at] if source is None else source.at[at],
            dst_ref=gathered.at[block, at],
            send_sem=sem.at[block, h],
            recv_sem=got.at[block, h],
            device_id={"ex": target},
            device_id_type=MESH,
        )

    across = me + 1 - 2 * y
    for h in range(parts):
        pl.when(z < depth - 1)(lambda: hop(me, h, sent_up, me + 2, q_hbm).start())
        pl.when(z > 0)(lambda: hop(me, h, sent_down, me - 2, q_hbm).start())
        hop(me, h, sent_across, across, q_hbm).start()

    spread = one_hot(
        iota((side, side), 1) == (iota((side, side), 0) % tiles) * per + iota((side, side), 0) // tiles
    )
    wide = one_hot(iota((side, LANES), 1) % side == iota((side, LANES), 0))
    right_cols = []
    for l in range(layers_here):
        ordered = dot(spread, l_ref[l]).astype(BF16)
        for low in range(per):
            col = iota((side, rows), 1)
            pick = one_hot(
                jnp.logical_and(
                    col % layers_here == l, iota((side, rows), 0) == (col // layers_here) * per + low
                )
            )
            at = (l * per + low) * side
            left_mat[at : at + side, :] = dot(ordered, pick).astype(BF16)
        tiled = dot(r_ref[l], wide)
        stack = jnp.concatenate([tiled] * (per * layers_here), axis=0)
        keep = iota(stack.shape, 0) // side == l * per + iota(stack.shape, 1) // side
        right_mat[:, l * LANES : (l + 1) * LANES] = jnp.where(keep, stack, 0.0).astype(BF16)

    batch = lifted.shape[0] // rows

    def lift(i, carry):
        at = pl.multiple_of(i * batch, batch)
        lifted[...] = raw[pl.ds(at, batch)].reshape(batch * rows, LANES).astype(F32)
        for r in range(rows):
            flat_stored[pl.ds(at, batch), r * LANES : (r + 1) * LANES] = lifted[
                pl.ds(r, batch, stride=rows), :
            ].astype(BF16)
        return carry

    per_raw = raw_rows // batch
    for i in range(n_raw):
        raw_copy(i).wait()
        lax.fori_loop(i * per_raw, (i + 1) * per_raw, lift, 0)

    def precondition(block, slot):
        lanes = [gathered[block, i] for i in range(per_block)]
        product = dot(left_mat[...], jnp.concatenate(lanes, axis=1))
        low = iota((side, LANES), 1) < side
        low_half = iota((tiles, LANES), 1) < side
        stacked = []
        for i in range(per_block):
            halves = []
            for l in range(layers_here):
                mine = product[l * per * side : (l + 1) * per * side, i * LANES : (i + 1) * LANES]
                both = jnp.where(low, mine[:side], mine[side:])
                both = both + pltpu.roll(both, side, 1)
                halves.append(jnp.where(low_half, both[:tiles], both[tiles:]).astype(BF16))
            stacked.append(jnp.concatenate(halves, axis=1))
        ready = dot(jnp.concatenate(stacked, axis=0), right_mat[...])
        for l in range(layers_here):
            ready_wide[l] = ready[:, l * LANES : (l + 1) * LANES]
        for c in range(tiles):
            for l in range(layers_here):
                at = (c * layers_here + l) * LANES
                ready_flat[slot * per_block : (slot + 1) * per_block, at : at + LANES] = ready_wide[
                    l, pl.ds(c, per_block, stride=tiles), :
                ].astype(BF16)

    def share(to):
        return pltpu.make_async_remote_copy(
            src_ref=partial.at[to],
            dst_ref=arrived.at[layer],
            send_sem=out_sem.at[to],
            recv_sem=in_sem.at[layer],
            device_id={"layer": to},
            device_id_type=MESH,
        )

    def compute(zz):
        for h in range(parts):
            hop(zz * 2 + 1 - y, h, sent_across, across).wait_recv()
        precondition(zz * 2, 0)
        precondition(zz * 2 + 1, 1)
        partial[zz] = lax.dot_general(
            ready_flat[...], flat_stored[...], (((1,), (1,)), ((), ())), preferred_element_type=F32
        )
        pl.when(zz != layer)(lambda: share(zz).start())

    def relay(distance):
        for h in range(parts):

            @pl.when(z >= distance)
            def _():
                block = me - 2 * distance
                hop(block, h, sent_up, me).wait_recv()
                pl.when(z < depth - 1)(lambda: hop(block, h, sent_up, me + 2).start())
                hop(block, h, sent_across, across).start()

            @pl.when(z + distance < depth)
            def _():
                block = me + 2 * distance
                hop(block, h, sent_down, me).wait_recv()
                pl.when(z > 0)(lambda: hop(block, h, sent_down, me - 2).start())
                hop(block, h, sent_across, across).start()

    own_copy.wait()

    def turn(i, carry):
        distance = (i + 1) // 2
        zz = jnp.where(i % 2 == 1, z - distance, z + distance)

        @pl.when(i % 2 == 0)
        def _():
            pl.when(distance + 1 < depth)(lambda: relay(distance + 1))

        pl.when(jnp.logical_and(zz >= 0, zz < depth))(lambda: compute(zz))
        return carry

    lax.fori_loop(0, 2 * depth - 1, turn, 0)

    total = partial[layer]
    for step in range(1, groups):
        other = lax.rem(layer + step, groups)
        pltpu.make_async_remote_copy(
            src_ref=partial.at[other],
            dst_ref=arrived.at[other],
            send_sem=out_sem.at[other],
            recv_sem=in_sem.at[other],
            device_id={"layer": other},
            device_id_type=MESH,
        ).wait_recv()
        total = total + arrived[other]
    out_ref[...] = total

    for step in range(1, groups):
        share(lax.rem(layer + step, groups)).wait_send()

    def drain(zz, carry):
        block = zz * 2 + y
        for h in range(parts):
            hop(block, h, sent_across, across).wait_send()
            up = jnp.logical_and(zz <= z, z < depth - 1)
            down = jnp.logical_and(zz >= z, z > 0)
            pl.when(up)(lambda: hop(block, h, sent_up, me + 2).wait_send())
            pl.when(down)(lambda: hop(block, h, sent_down, me - 2).wait_send())
        return carry

    lax.fori_loop(0, depth, drain, 0)


def rows_of(array, side):
    count, layers_here, size = array.shape
    tiles = size // LANES
    split = array.reshape(count, layers_here, tiles, LANES).transpose(0, 2, 1, 3)
    return split.reshape(count, tiles * layers_here, LANES)


def shards(groups, ex, queries, stored, left_inv, right_inv):
    per_block, layers_here, size = queries.shape
    side = left_inv.shape[1]
    stored_rows = stored.shape[0]
    per = LANES // side
    rows = size // LANES * layers_here
    parts = 2
    batch = 16
    n_raw = 4
    dma = pltpu.SemaphoreType.DMA
    return pl.pallas_call(
        functools.partial(kernel, groups, ex, per_block, layers_here, side, parts),
        out_shape=jax.ShapeDtypeStruct((2 * per_block, stored_rows), F32),
        in_specs=[pl.BlockSpec(memory_space=pl.ANY)] * 2 + [pl.BlockSpec(memory_space=pltpu.VMEM)] * 2,
        out_specs=pl.BlockSpec(memory_space=pltpu.VMEM),
        scratch_shapes=[
            pltpu.VMEM((ex, per_block, rows, LANES), BF16),
            pltpu.VMEM((stored_rows, rows, LANES), BF16),
            pltpu.VMEM((stored_rows, rows * LANES), BF16),
            pltpu.VMEM((batch * rows, LANES), F32),
            pltpu.VMEM((layers_here * per * side, rows), BF16),
            pltpu.VMEM((layers_here * LANES, layers_here * LANES), BF16),
            pltpu.VMEM((layers_here, per_block * size // LANES, LANES), F32),
            pltpu.VMEM((2 * per_block, rows * LANES), BF16),
            pltpu.VMEM((groups, 2 * per_block, stored_rows), F32),
            pltpu.VMEM((groups, 2 * per_block, stored_rows), F32),
            dma((ex, parts)),
            dma((ex, parts)),
            dma((ex, parts)),
            dma((ex, parts)),
            dma,
            dma((n_raw,)),
            dma((groups,)),
            dma((groups,)),
        ],
        compiler_params=pltpu.CompilerParams(
            collective_id=0, has_side_effects=True, vmem_limit_bytes=60 << 20
        ),
    )(rows_of(queries, side), rows_of(stored, side), left_inv, right_inv)


def solution(mesh):
    placed = (
        P("ex", "layer", None),
        P("ex", "layer", None),
        P("layer", None, None),
        P("layer", None, None),
    )
    groups, ex = mesh.shape["layer"], mesh.shape["ex"]
    return jax.shard_map(
        functools.partial(shards, groups, ex),
        mesh=mesh, in_specs=placed, out_specs=P("layer", "ex"), check_vma=False,
    )
```

time: 92.8 us -> 45.5 us (0.49)
  the two profiles are of different devices: /device:TPU:0 before, /device:TPU:24 now
where the time goes in v1:
time: 45.5 us; the launch traced here: 45.3 us
  Pallas kernels  43.9 us (96%)
  local copies, waits for them, and re-layouts  1.38 us (3%)
    pallas_call x1, Pallas kernels, shards(): pl.pallas_call(functools.partial(kernel, groups, ex, per_block, layers_he...  43.9 us
    unnamed x1, local copies, waits for them, and re-layouts  1.38 us

profile of v1, /device:TPU:24, one launch (start us, length us, event | category | flops | bytes accessed | tf_op | source)
XLA Modules:
  0.0 45.3 jit_solution(13825492699854722351)
XLA Ops:
  0.0 43.9 %shard_map.46 = f32[32,256]{1,0:T(8,128)} custom-call(bf16[16,64,128]{2,1,0:T(8,128)(2,1)} %bitcast.11, bf16[256,64,128]{2,1,0:T(8,128)(2,1)} %bitcast.10, bf16[2,64,64]{2,1,0:T(8,128)(2,1)} %l_ref.1, bf16[2,64,64]{2,1,0:T(8,128)(2,1)} %r_ref.1), custom_call_target="tpu_custom_call" | custom-call | tf_op jit(solution)/shard_map/pallas_call | solution.py:248
  43.9 1.4 %copy.8 = f32[32,256]{1,0:T(8,128)} copy(f32[32,256]{1,0:T(8,128)} %shard_map.46) | data formatting | bytes 65536

commit v2 on v1

--- a/solution.py
+++ b/solution.py
@@ -26,9 +26,9 @@
 
 
 def kernel(
-    groups, ex, per_block, layers_here, side, parts,
+    groups, ex, per_block, layers_here, side, cuts, batch,
     q_hbm, s_hbm, l_ref, r_ref, out_ref,
-    gathered, raw, flat_stored, lifted, left_mat, right_mat, ready_wide, ready_flat,
+    gathered, raw, flat_stored, left_mat, right_mat, ready_flat,
     partial, arrived,
     got, sent_up, sent_down, sent_across, own_sem, raw_sem, out_sem, in_sem,
 ):
@@ -39,7 +39,8 @@
     per = LANES // side
     tiles = side // per
     rows = tiles * layers_here
-    piece = per_block // parts
+    parts = len(cuts) - 1
+    last = parts - 1
 
     barrier = pltpu.get_barrier_semaphore()
 
@@ -69,7 +70,7 @@
     pl.semaphore_wait(barrier, here + groups)
 
     def hop(block, h, sem, target, source=None):
-        at = pl.ds(h * piece, piece)
+        at = pl.ds(cuts[h], cuts[h + 1] - cuts[h])
         return pltpu.make_async_remote_copy(
             src_ref=gathered.at[block, at] if source is None else source.at[at],
             dst_ref=gathered.at[block, at],
@@ -80,10 +81,12 @@
         )
 
     across = me + 1 - 2 * y
+    hop(me, last, sent_across, across, q_hbm).start()
     for h in range(parts):
         pl.when(z < depth - 1)(lambda: hop(me, h, sent_up, me + 2, q_hbm).start())
         pl.when(z > 0)(lambda: hop(me, h, sent_down, me - 2, q_hbm).start())
-        hop(me, h, sent_across, across, q_hbm).start()
+        if h < last:
+            hop(me, h, sent_across, across, q_hbm).start()
 
     spread = one_hot(
         iota((side, side), 1) == (iota((side, side), 0) % tiles) * per + iota((side, side), 0) // tiles
@@ -106,15 +109,12 @@
         keep = iota(stack.shape, 0) // side == l * per + iota(stack.shape, 1) // side
         right_mat[:, l * LANES : (l + 1) * LANES] = jnp.where(keep, stack, 0.0).astype(BF16)
 
-    batch = lifted.shape[0] // rows
 
     def lift(i, carry):
         at = pl.multiple_of(i * batch, batch)
-        lifted[...] = raw[pl.ds(at, batch)].reshape(batch * rows, LANES).astype(F32)
+        turned = jnp.swapaxes(raw[pl.ds(at, batch)], 0, 1)
         for r in range(rows):
-            flat_stored[pl.ds(at, batch), r * LANES : (r + 1) * LANES] = lifted[
-                pl.ds(r, batch, stride=rows), :
-            ].astype(BF16)
+            flat_stored[pl.ds(at, batch), r * LANES : (r + 1) * LANES] = turned[r]
         return carry
 
     per_raw = raw_rows // batch
@@ -137,14 +137,10 @@
                 halves.append(jnp.where(low_half, both[:tiles], both[tiles:]).astype(BF16))
             stacked.append(jnp.concatenate(halves, axis=1))
         ready = dot(jnp.concatenate(stacked, axis=0), right_mat[...])
-        for l in range(layers_here):
-            ready_wide[l] = ready[:, l * LANES : (l + 1) * LANES]
+        wide_at = layers_here * LANES
+        turned = jnp.swapaxes(ready.astype(BF16).reshape(per_block, tiles, wide_at), 0, 1)
         for c in range(tiles):
-            for l in range(layers_here):
-                at = (c * layers_here + l) * LANES
-                ready_flat[slot * per_block : (slot + 1) * per_block, at : at + LANES] = ready_wide[
-                    l, pl.ds(c, per_block, stride=tiles), :
-                ].astype(BF16)
+            ready_flat[slot * per_block : (slot + 1) * per_block, c * wide_at : (c + 1) * wide_at] = turned[c]
 
     def share(to):
         return pltpu.make_async_remote_copy(
@@ -157,39 +153,49 @@
         )
 
     def compute(zz):
+        precondition(zz * 2 + y, 0)
+        other = zz * 2 + 1 - y
         for h in range(parts):
-            hop(zz * 2 + 1 - y, h, sent_across, across).wait_recv()
-        precondition(zz * 2, 0)
-        precondition(zz * 2 + 1, 1)
-        partial[zz] = lax.dot_general(
+            if h < last:
+                hop(other, h, sent_across, across).wait_recv()
+        precondition(other, 1)
+        scores = lax.dot_general(
             ready_flat[...], flat_stored[...], (((1,), (1,)), ((), ())), preferred_element_type=F32
         )
+        partial[zz, pl.ds(pl.multiple_of(y * per_block, per_block), per_block)] = scores[:per_block]
+        partial[zz, pl.ds(pl.multiple_of((1 - y) * per_block, per_block), per_block)] = scores[per_block:]
         pl.when(zz != layer)(lambda: share(zz).start())
 
+    def onward(block, h, upward):
+        if upward:
+            pl.when(z < depth - 1)(lambda: hop(block, h, sent_up, me + 2).start())
+        else:
+            pl.when(z > 0)(lambda: hop(block, h, sent_down, me - 2).start())
+
     def relay(distance):
-        for h in range(parts):
-
-            @pl.when(z >= distance)
-            def _():
-                block = me - 2 * distance
-                hop(block, h, sent_up, me).wait_recv()
-                pl.when(z < depth - 1)(lambda: hop(block, h, sent_up, me + 2).start())
-                hop(block, h, sent_across, across).start()
-
-            @pl.when(z + distance < depth)
-            def _():
-                block = me + 2 * distance
-                hop(block, h, sent_down, me).wait_recv()
-                pl.when(z > 0)(lambda: hop(block, h, sent_down, me - 2).start())
-                hop(block, h, sent_across, across).start()
-
+        for h in range(parts + 1):
+            for upward in (True, False):
+
+                @pl.when(z >= distance if upward else z + distance < depth)
+                def _():
+                    offset = -2 * distance if upward else 2 * distance
+                    block = (me if h < parts else across) + offset
+                    piece = min(h, last)
+                    hop(block, piece, sent_up, me).wait_recv()
+                    onward(block, piece, upward)
+                    if h < last:
+                        hop(block, h, sent_across, across).start()
+
+    hop(across, last, sent_across, across).wait_recv()
+    onward(across, last, True)
+    onward(across, last, False)
     own_copy.wait()
 
     def turn(i, carry):
         distance = (i + 1) // 2
         zz = jnp.where(i % 2 == 1, z - distance, z + distance)
 
-        @pl.when(i % 2 == 0)
+        @pl.when(jnp.logical_or(i == 0, i % 2 == 1))
         def _():
             pl.when(distance + 1 < depth)(lambda: relay(distance + 1))
 
@@ -216,16 +222,19 @@
         share(lax.rem(layer + step, groups)).wait_send()
 
     def drain(zz, carry):
-        block = zz * 2 + y
-        for h in range(parts):
-            hop(block, h, sent_across, across).wait_send()
-            up = jnp.logical_and(zz <= z, z < depth - 1)
-            down = jnp.logical_and(zz >= z, z > 0)
-            pl.when(up)(lambda: hop(block, h, sent_up, me + 2).wait_send())
-            pl.when(down)(lambda: hop(block, h, sent_down, me - 2).wait_send())
+        up = jnp.logical_and(zz <= z, z < depth - 1)
+        down = jnp.logical_and(zz >= z, z > 0)
+        for h in range(parts + 1):
+            block = zz * 2 + (y if h < parts else 1 - y)
+            piece = min(h, last)
+            if h < last:
+                hop(block, h, sent_across, across).wait_send()
+            pl.when(up)(lambda: hop(block, piece, sent_up, me + 2).wait_send())
+            pl.when(down)(lambda: hop(block, piece, sent_down, me - 2).wait_send())
         return carry
 
     lax.fori_loop(0, depth, drain, 0)
+    hop(me, last, sent_across, across).wait_send()
 
 
 def rows_of(array, side):
@@ -241,12 +250,14 @@
     stored_rows = stored.shape[0]
     per = LANES // side
     rows = size // LANES * layers_here
-    parts = 2
+    detour = max(1, per_block * 3 // 16)
+    cuts = (0, (per_block - detour + 1) // 2, per_block - detour, per_block)
+    parts = len(cuts) - 1
     batch = 16
     n_raw = 4
     dma = pltpu.SemaphoreType.DMA
     return pl.pallas_call(
-        functools.partial(kernel, groups, ex, per_block, layers_here, side, parts),
+        functools.partial(kernel, groups, ex, per_block, layers_here, side, cuts, batch),
         out_shape=jax.ShapeDtypeStruct((2 * per_block, stored_rows), F32),
         in_specs=[pl.BlockSpec(memory_space=pl.ANY)] * 2 + [pl.BlockSpec(memory_space=pltpu.VMEM)] * 2,
         out_specs=pl.BlockSpec(memory_space=pltpu.VMEM),
@@ -254,10 +265,8 @@
             pltpu.VMEM((ex, per_block, rows, LANES), BF16),
             pltpu.VMEM((stored_rows, rows, LANES), BF16),
             pltpu.VMEM((stored_rows, rows * LANES), BF16),
-            pltpu.VMEM((batch * rows, LANES), F32),
             pltpu.VMEM((layers_here * per * side, rows), BF16),
             pltpu.VMEM((layers_here * LANES, layers_here * LANES), BF16),
-            pltpu.VMEM((layers_here, per_block * size // LANES, LANES), F32),
             pltpu.VMEM((2 * per_block, rows * LANES), BF16),
             pltpu.VMEM((groups, 2 * per_block, stored_rows), F32),
             pltpu.VMEM((groups, 2 * per_block, stored_rows), F32),

time: 45.5 us -> 38.3 us (0.84)
  the two profiles are of different devices: /device:TPU:24 before, /device:TPU:0 now
where the time goes in v2:
time: 38.3 us; the launch traced here: 38.1 us
  Pallas kernels  36.7 us (96%)
  local copies, waits for them, and re-layouts  1.38 us (4%)
    pallas_call x1, Pallas kernels, shards(): pl.pallas_call(functools.partial(kernel, groups, ex, per_block, layers_he...  36.7 us
    unnamed x1, local copies, waits for them, and re-layouts  1.38 us

profile of v2, /device:TPU:0, one launch (start us, length us, event | category | flops | bytes accessed | tf_op | source)
XLA Modules:
  0.0 38.1 jit_solution(13159059700721039207)
XLA Ops:
  0.0 36.7 %shard_map.46 = f32[32,256]{1,0:T(8,128)} custom-call(bf16[16,64,128]{2,1,0:T(8,128)(2,1)} %bitcast.11, bf16[256,64,128]{2,1,0:T(8,128)(2,1)} %bitcast.10, bf16[2,64,64]{2,1,0:T(8,128)(2,1)} %l_ref.1, bf16[2,64,64]{2,1,0:T(8,128)(2,1)} %r_ref.1), custom_call_target="tpu_custom_call" | custom-call | tf_op jit(solution)/shard_map/pallas_call | solution.py:259
  36.7 1.4 %copy.8 = f32[32,256]{1,0:T(8,128)} copy(f32[32,256]{1,0:T(8,128)} %shard_map.46) | data formatting | bytes 65536

commit v3 on v2

--- a/solution.py
+++ b/solution.py
@@ -122,7 +122,7 @@
         raw_copy(i).wait()
         lax.fori_loop(i * per_raw, (i + 1) * per_raw, lift, 0)
 
-    def precondition(block, slot):
+    def precondition(block, slot, ready_flat):
         lanes = [gathered[block, i] for i in range(per_block)]
         product = dot(left_mat[...], jnp.concatenate(lanes, axis=1))
         low = iota((side, LANES), 1) < side
@@ -152,19 +152,21 @@
             device_id_type=MESH,
         )
 
-    def compute(zz):
-        precondition(zz * 2 + y, 0)
+    def work(stage, zz, flat):
         other = zz * 2 + 1 - y
-        for h in range(parts):
-            if h < last:
+        if stage == 0:
+            precondition(zz * 2 + y, 0, flat)
+        elif stage == 1:
+            for h in range(last):
                 hop(other, h, sent_across, across).wait_recv()
-        precondition(other, 1)
-        scores = lax.dot_general(
-            ready_flat[...], flat_stored[...], (((1,), (1,)), ((), ())), preferred_element_type=F32
-        )
-        partial[zz, pl.ds(pl.multiple_of(y * per_block, per_block), per_block)] = scores[:per_block]
-        partial[zz, pl.ds(pl.multiple_of((1 - y) * per_block, per_block), per_block)] = scores[per_block:]
-        pl.when(zz != layer)(lambda: share(zz).start())
+            precondition(other, 1, flat)
+        elif stage == 2:
+            scores = lax.dot_general(
+                flat[...], flat_stored[...], (((1,), (1,)), ((), ())), preferred_element_type=F32
+            )
+            partial[zz, pl.ds(pl.multiple_of(y * per_block, per_block), per_block)] = scores[:per_block]
+            partial[zz, pl.ds(pl.multiple_of((1 - y) * per_block, per_block), per_block)] = scores[per_block:]
+            pl.when(zz != layer)(lambda: share(zz).start())
 
     def onward(block, h, upward):
         if upward:
@@ -172,37 +174,34 @@
         else:
             pl.when(z > 0)(lambda: hop(block, h, sent_down, me - 2).start())
 
-    def relay(distance):
-        for h in range(parts + 1):
-            for upward in (True, False):
-
-                @pl.when(z >= distance if upward else z + distance < depth)
-                def _():
-                    offset = -2 * distance if upward else 2 * distance
-                    block = (me if h < parts else across) + offset
-                    piece = min(h, last)
-                    hop(block, piece, sent_up, me).wait_recv()
-                    onward(block, piece, upward)
-                    if h < last:
-                        hop(block, h, sent_across, across).start()
+    def relay(h, distance):
+        for upward in (True, False):
+
+            @pl.when(z >= distance if upward else z + distance < depth)
+            def _():
+                offset = -2 * distance if upward else 2 * distance
+                block = (me if h < parts else across) + offset
+                piece = min(h, last)
+                hop(block, piece, sent_up, me).wait_recv()
+                onward(block, piece, upward)
+                if h < last:
+                    hop(block, h, sent_across, across).start()
 
     hop(across, last, sent_across, across).wait_recv()
     onward(across, last, True)
     onward(across, last, False)
     own_copy.wait()
 
-    def turn(i, carry):
-        distance = (i + 1) // 2
-        zz = jnp.where(i % 2 == 1, z - distance, z + distance)
-
-        @pl.when(jnp.logical_or(i == 0, i % 2 == 1))
-        def _():
-            pl.when(distance + 1 < depth)(lambda: relay(distance + 1))
-
-        pl.when(jnp.logical_and(zz >= 0, zz < depth))(lambda: compute(zz))
+    def turn(distance, carry):
+        below = z >= distance
+        above = jnp.logical_and(distance > 0, z + distance < depth)
+        for h in range(parts + 1):
+            relay(h, distance + 1)
+            pl.when(below)(lambda: work(h, z - distance, ready_flat.at[0]))
+            pl.when(above)(lambda: work(h, z + distance, ready_flat.at[1]))
         return carry
 
-    lax.fori_loop(0, 2 * depth - 1, turn, 0)
+    lax.fori_loop(0, depth, turn, 0)
 
     total = partial[layer]
     for step in range(1, groups):
@@ -250,7 +249,7 @@
     stored_rows = stored.shape[0]
     per = LANES // side
     rows = size // LANES * layers_here
-    detour = max(1, per_block * 3 // 16)
+    detour = max(1, per_block // 8)
     cuts = (0, (per_block - detour + 1) // 2, per_block - detour, per_block)
     parts = len(cuts) - 1
     batch = 16
@@ -267,7 +266,7 @@
             pltpu.VMEM((stored_rows, rows * LANES), BF16),
             pltpu.VMEM((layers_here * per * side, rows), BF16),
             pltpu.VMEM((layers_here * LANES, layers_here * LANES), BF16),
-            pltpu.VMEM((2 * per_block, rows * LANES), BF16),
+            pltpu.VMEM((2, 2 * per_block, rows * LANES), BF16),
             pltpu.VMEM((groups, 2 * per_block, stored_rows), F32),
             pltpu.VMEM((groups, 2 * per_block, stored_rows), F32),
             dma((ex, parts)),

time: 38.3 us -> 37.1 us (0.969)
  Pallas kernels: 36.7 us -> 35.5 us
    pallas_call x1, Pallas kernels: 36.7 us -> 35.5 us  [shards(): pl.pallas_call(functools.partial(kernel, groups, ex, per_block, layers_he...]
where the time goes in v3:
time: 37.1 us; the launch traced here: 36.9 us
  Pallas kernels  35.5 us (96%)
  local copies, waits for them, and re-layouts  1.38 us (4%)
    pallas_call x1, Pallas kernels, shards(): pl.pallas_call(functools.partial(kernel, groups, ex, per_block, layers_he...  35.5 us
    unnamed x1, local copies, waits for them, and re-layouts  1.38 us

profile of v3, /device:TPU:0, one launch (start us, length us, event | category | flops | bytes accessed | tf_op | source)
XLA Modules:
  0.0 36.9 jit_solution(12030369258580259320)
XLA Ops:
  0.0 35.5 %shard_map.46 = f32[32,256]{1,0:T(8,128)} custom-call(bf16[16,64,128]{2,1,0:T(8,128)(2,1)} %bitcast.11, bf16[256,64,128]{2,1,0:T(8,128)(2,1)} %bitcast.10, bf16[2,64,64]{2,1,0:T(8,128)(2,1)} %l_ref.1, bf16[2,64,64]{2,1,0:T(8,128)(2,1)} %r_ref.1), custom_call_target="tpu_custom_call" | custom-call | tf_op jit(solution)/shard_map/pallas_call | solution.py:258
  35.5 1.4 %copy.8 = f32[32,256]{1,0:T(8,128)} copy(f32[32,256]{1,0:T(8,128)} %shard_map.46) | data formatting | bytes 65536
